TPU v7x, 32 devices: a whole 2x2x4 slice. The times are simulated.
32 devices in a mesh: tm: 16 (over z, y, x), col: 2 (over core).
Axes of the slice: x: 2, y: 2, z: 4, core: 2. Of those that a mesh axis runs over, the one named last changes fastest.
Arguments:
- initial_state: float32 [1024], replicated, may hold values from -6 to 6
- coupling: float32 [1024, 1024], replicated, may hold values from -0.1875 to 0.1875
- modulation: float32 [1024, 1024], replicated, may hold values from -0.1875 to 0.1875
- gains: float32 [16, 5], P('tm'), may hold values from -1 to 1
- forcing: float32 [16, 5, 1024], P('tm'), may hold values from -6 to 6
Outputs:
- slab_ends: float32 [16, 1024], P('tm', 'col')
All inputs are finite; a program needn't handle non-finite values.
Results may differ from a plain program's by a relative error of at most 0.0003.
Values sent between devices are 32-bit elements; how exact they have to be, the bound alone decides.
A program may use at most 128 MiB of HBM per device.

v0:
```python
import functools

import jax
import jax.numpy as jnp
from jax import lax
from jax.experimental import pallas as pl
from jax.experimental.pallas import tpu as pltpu
from jax.sharding import PartitionSpec as P

step_size = 0.1
highest = lax.Precision.HIGHEST
MESH = pl.DeviceIdType.MESH
f32, bf16 = jnp.float32, jnp.bfloat16


def group_width(devices):
    width = 1
    while width * width < devices:
        width *= 2
    return width


def kernel(
    width, cores, y0_ref, c_hbm, m_hbm, gains_ref, forcing_ref, out_ref,
    cbuf, mbuf, bt, vt, wa_hi, wa_lo, wb_hi, wb_lo, wc_hi, wc_lo,
    x, acc, xs0, xs1, zs, gbuf, fbuf, chain_in, out_in, psend, yv,
    csem, gsend, grecv, vsend, fsend, frecv, chain_send, chain_recv, out_send, out_recv,
):
    rows, size = x.shape
    slabs = zs.shape[0]
    nodes = forcing_ref.shape[1]
    steps = (nodes - 1) // 2
    half = out_ref.shape[1]
    window = chain_in.shape[2]
    tile = min(256, size)
    devices = lax.axis_size("tm") * cores
    groups = devices // width
    me_tm, me_col = lax.axis_index("tm"), lax.axis_index("col")
    flat = me_tm * cores + me_col
    g = flat // width
    p = flat % width
    local = me_tm % slabs
    is_head = g == 0
    is_vec = jnp.logical_and(is_head, p < groups)

    def dev(index):
        return {"tm": index // cores, "col": index % cores}

    def remote(src, dst, send, recv, index):
        return pltpu.make_async_remote_copy(
            src_ref=src, dst_ref=dst, send_sem=send, recv_sem=recv,
            device_id=dev(index), device_id_type=MESH,
        )

    load_c = pltpu.make_async_copy(c_hbm, cbuf, csem.at[0])
    load_m = pltpu.make_async_copy(m_hbm, mbuf, csem.at[1])
    load_c.start()
    load_m.start()

    gbuf[...] = jnp.zeros_like(gbuf)
    fbuf[...] = jnp.zeros_like(fbuf)

    barrier = pltpu.get_barrier_semaphore()

    @pl.loop(1, devices)
    def _(o):
        pl.semaphore_signal(barrier, inc=1, device_id=dev((flat + o) % devices), device_id_type=MESH)

    pl.semaphore_wait(barrier, devices - 1)

    def mate_gain(o):
        target = (g * slabs + (local + o) % slabs) * cores + me_col
        return remote(gains_ref, gbuf.at[local], gsend.at[o], grecv.at[local], target)

    def vec_gain():
        return remote(gains_ref, gbuf.at[local], vsend.at[0], grecv.at[local], g)

    def vec_force():
        return remote(forcing_ref.at[0], fbuf.at[local], fsend.at[0], frecv.at[local], g)

    feeds_vec = jnp.logical_and(me_col == 0, flat != 0)

    @pl.when(jnp.logical_not(is_head))
    def _():
        gbuf[local] = gains_ref[...]
        for o in range(1, slabs):
            mate_gain(o).start()

    @pl.when(feeds_vec)
    def _():
        vec_gain().start()
        vec_force().start()

    @pl.when(flat == 0)
    def _():
        gbuf[0] = gains_ref[...]
        fbuf[0] = forcing_ref[0]

    row_id = lax.broadcasted_iota(jnp.int32, (rows, tile), 0)
    col_id = lax.broadcasted_iota(jnp.int32, (rows, tile), 1)

    for n in range(size // tile):
        ns = slice(n * tile, (n + 1) * tile)
        eye = jnp.where(col_id + n * tile == row_id + p * rows, 1.0, 0.0).astype(f32)
        first = jnp.where(jnp.logical_and(row_id == 0, p == 0), y0_ref[:, ns], 0.0)
        start = jnp.where(is_head, first, eye)
        x[:, ns] = start
        hi = start.astype(bf16)
        xs0[:rows, ns] = hi
        xs0[rows:, ns] = (start - hi.astype(f32)).astype(bf16)

    def skew(src, dst):
        @pl.loop(0, size // 128)
        def _(i):
            blk = pl.ds(pl.multiple_of(i * 128, 128), 128)
            dst[blk, :] = src[:, blk].T - src[blk, :]

    load_c.wait()
    skew(cbuf, bt)
    load_m.wait()
    skew(mbuf, vt)

    for i in range(slabs):
        @pl.when(jnp.logical_or(
            jnp.logical_and(jnp.logical_not(is_head), local != i),
            jnp.logical_and(is_vec, flat + i != 0),
        ))
        def _(i=i):
            remote(gains_ref, gbuf.at[i], gsend.at[0], grecv.at[i], 0).wait_recv()

        @pl.when(jnp.logical_and(is_vec, flat + i != 0))
        def _(i=i):
            remote(forcing_ref.at[0], fbuf.at[i], fsend.at[0], frecv.at[i], 0).wait_recv()

    pieces = max(1, size // 128)

    def form(ns, gain, w_hi, w_lo):
        for k in range(pieces):
            ks = slice(k * size // pieces, (k + 1) * size // pieces)
            w = bt[ks, ns] + gain * vt[ks, ns]
            hi = w.astype(bf16)
            w_hi[ks, ns] = hi
            w_lo[ks, ns] = (w - hi.astype(f32)).astype(bf16)

    wa, wb, wc = (wa_hi, wa_lo), (wb_hi, wb_lo), (wc_hi, wc_lo)

    def gain_of(slab, node):
        return gbuf[slab][:, node:node + 1]

    @pl.loop(0, size // tile)
    def _(n):
        form(pl.ds(pl.multiple_of(n * tile, tile), tile), gain_of(0, 0), *wc)

    h = step_size
    push = jnp.logical_and(row_id == 0, is_head)

    def stage(slab, kind, node, w, source, target, following):
        @pl.loop(0, size // tile)
        def _(n):
            ns = pl.ds(pl.multiple_of(n * tile, tile), tile)
            both = jnp.dot(source[...], w[0][:, ns], preferred_element_type=f32)
            k = both[:rows] + both[rows:]
            k = k + jnp.dot(source[:rows, :], w[1][:, ns], preferred_element_type=f32)
            k = k + jnp.where(push, fbuf[slab, node:node + 1, ns], 0.0)
            now = x[:, ns]
            if kind == 0:
                acc[:, ns] = now + (h / 6.0) * k
                arg = now + (0.5 * h) * k
            elif kind == 1:
                acc[:, ns] += (h / 3.0) * k
                arg = now + (0.5 * h) * k
            elif kind == 2:
                acc[:, ns] += (h / 3.0) * k
                arg = now + h * k
            else:
                arg = acc[:, ns] + (h / 6.0) * k
                x[:, ns] = arg
                if node == nodes - 1:
                    zs[slab, :, ns] = arg
            hi = arg.astype(bf16)
            target[:rows, ns] = hi
            target[rows:, ns] = (arg - hi.astype(f32)).astype(bf16)
            if following is not None:
                form(ns, following[0], *following[1])

    @pl.loop(0, slabs)
    def _(slab):
        after = jnp.minimum(slab + 1, slabs - 1)
        for step in range(steps):
            w0 = wc if step == 0 else wa
            base = 2 * step
            last = step == steps - 1
            stage(slab, 0, base, w0, xs0, xs1, (gain_of(slab, base + 1), wb) if step == 0 else None)
            stage(slab, 1, base + 1, wb, xs1, xs0, (gain_of(slab, base + 2), wa))
            stage(slab, 2, base + 1, wb, xs0, xs1, None)
            stage(slab, 3, base + 2, wa, xs1, xs0, (gain_of(after, 0), wc) if last else (gain_of(slab, base + 3), wb))

    def start_of(q):
        return q * rows // 128 * 128

    def to_chain(q):
        slot = jnp.where(is_head, width, p)
        index = jnp.where(is_head, p + 1, g + 1) * width + q
        src = psend.at[slabs - 1, :, pl.ds(start_of(q), window)]
        return remote(src, chain_in.at[slot], chain_send.at[q], chain_recv.at[slot], index)

    def to_out(o):
        d = (p + o) % width
        src = psend.at[d // cores, :, pl.ds(pl.multiple_of(d % cores * half, half), half)]
        return remote(src, out_in.at[p], out_send.at[o], out_recv.at[p], g * width + d)

    def head_out(d):
        src = psend.at[d // cores, :, pl.ds(d % cores * half, half)]
        return remote(src, out_in.at[width], out_send.at[d], out_recv.at[width], p * width + d)

    def chain_wait(slot):
        remote(psend.at[0, :, pl.ds(0, window)], chain_in.at[slot], chain_send.at[0], chain_recv.at[slot], 0).wait_recv()

    def out_wait(slot):
        remote(psend.at[0, :, pl.ds(0, half)], out_in.at[slot], out_send.at[0], out_recv.at[slot], 0).wait_recv()

    @pl.when(is_vec)
    def _():
        for s in range(slabs):
            psend[s] = zs[s, 0:1, :]

        @pl.when(p + 1 < groups)
        def _():
            for q in range(width):
                to_chain(q).start()

        for d in range(width):
            if d == 0:
                @pl.when(p == 0)
                def _():
                    out_in[width] = psend[0][:, :half]

                @pl.when(p != 0)
                def _():
                    head_out(0).start()
            else:
                head_out(d).start()

    @pl.when(is_head)
    def _():
        @pl.when(p != 0)
        def _():
            out_wait(width)

        out_ref[...] = out_in[width]

    @pl.when(jnp.logical_not(is_head))
    def _():
        chain_wait(width)
        yv[...] = chain_in[width]

        @pl.when(g > 1)
        def _():
            for q in range(width):
                chain_wait(q)
            total = yv[...]
            for q in range(width):
                total = total + chain_in[q]
            yv[...] = total

        begin = yv[...]
        if rows < window:
            part = begin[:, :rows]
            for i in range(1, window // rows):
                part = jnp.where(p % (window // rows) == i, begin[:, i * rows:(i + 1) * rows], part)
            begin = part
        begin = jnp.broadcast_to(begin, (8, rows))

        def apply_map(s):
            psend[s] = jnp.dot(begin, zs[s], precision=highest, preferred_element_type=f32)[0:1, :]

        apply_map(slabs - 1)

        @pl.when(g + 1 < groups)
        def _():
            for q in range(width):
                to_chain(q).start()

        for s in range(slabs - 1):
            apply_map(s)
        for o in range(1, width):
            to_out(o).start()
        own = psend[p // cores]
        mine = own[:, :half]
        for c in range(1, cores):
            mine = jnp.where(me_col == c, own[:, c * half:(c + 1) * half], mine)
        out_wait(width)
        mine = mine + out_in[width]
        for o in range(1, width):
            q = (p + o) % width
            out_wait(q)
            mine = mine + out_in[q]
        out_ref[...] = mine
        for o in range(1, width):
            to_out(o).wait_send()
        for o in range(1, slabs):
            mate_gain(o).wait_send()

        @pl.when(g + 1 < groups)
        def _():
            for q in range(width):
                to_chain(q).wait_send()

    @pl.when(is_vec)
    def _():
        @pl.when(p + 1 < groups)
        def _():
            for q in range(width):
                to_chain(q).wait_send()

        @pl.when(p != 0)
        def _():
            head_out(0).wait_send()

        for d in range(1, width):
            head_out(d).wait_send()

    @pl.when(feeds_vec)
    def _():
        vec_gain().wait_send()
        vec_force().wait_send()


def shards(initial_state, coupling, modulation, gains, forcing):
    size = coupling.shape[0]
    cores = lax.axis_size("col")
    devices = lax.axis_size("tm") * cores
    width = group_width(devices)
    rows = size // width
    slabs = width // cores
    nodes = gains.shape[1]
    half = size // cores
    window = max(128, rows)
    vmem = pltpu.VMEM
    dma = pltpu.SemaphoreType.DMA
    mat32, mat16 = vmem((size, size), f32), vmem((size, size), bf16)
    return pl.pallas_call(
        functools.partial(kernel, width, cores),
        out_shape=jax.ShapeDtypeStruct((1, half), f32),
        in_specs=[
            pl.BlockSpec(memory_space=vmem),
            pl.BlockSpec(memory_space=pl.ANY),
            pl.BlockSpec(memory_space=pl.ANY),
            pl.BlockSpec(memory_space=vmem),
            pl.BlockSpec(memory_space=vmem),
        ],
        out_specs=pl.BlockSpec(memory_space=vmem),
        scratch_shapes=[
            mat32, mat32, mat32, mat32,
            mat16, mat16, mat16, mat16, mat16, mat16,
            vmem((rows, size), f32),
            vmem((rows, size), f32),
            vmem((2 * rows, size), bf16),
            vmem((2 * rows, size), bf16),
            vmem((slabs, rows, size), f32),
            vmem((slabs, 1, nodes), f32),
            vmem((slabs, nodes, size), f32),
            vmem((width + 1, 1, window), f32),
            vmem((width + 1, 1, half), f32),
            vmem((slabs, 1, size), f32),
            vmem((1, window), f32),
            dma((2,)), dma((slabs,)), dma((slabs,)), dma((1,)), dma((1,)), dma((slabs,)),
            dma((width,)), dma((width + 1,)), dma((width,)), dma((width + 1,)),
        ],
        compiler_params=pltpu.CompilerParams(
            collective_id=0, has_side_effects=True, vmem_limit_bytes=60 * 1024 * 1024
        ),
    )(initial_state[None, :], coupling, modulation, gains, forcing)


def solution(mesh):
    in_specs = (P(), P(), P(), P("tm", None), P("tm", None, None))
    out_specs = P("tm", "col")
    return jax.shard_map(shards, mesh=mesh, in_specs=in_specs, out_specs=out_specs, check_vma=False)
```

profile of v0, /device:TPU:25, one launch (start us, length us, event | category | flops | bytes accessed | tf_op | source)
XLA Modules:
  0.0 97.0 jit_solution(13818587119603914683)
XLA Ops:
  0.0 1.3 %copy.6.forcing_ref = f32[1,5,1024]{2,1,0:T(8,128)} copy(f32[1,5,1024]{2,0,1:T(1,128)} %param.9) | data formatting | bytes 40960 | tf_op args[4]
  1.3 94.4 %shard_map.55 = f32[1,512]{1,0:T(1,128)} custom-call(f32[1,1024]{1,0:T(1,128)} %bitcast.1, f32[1024,1024]{1,0:T(8,128)} %c_hbm.1, f32[1024,1024]{1,0:T(8,128)} %m_hbm.1, f32[1,5]{1,0:T(1,128)} %gains_ref.1, f32[1,5,1024]{2,1,0:T(8,128)} %copy.6.forcing_ref), custom_call_target="tpu_custom_call" | custom-call | tf_op jit(solution)/shard_map/pallas_call | solution.py:342
  95.7 1.2 %copy.8 = f32[1,512]{1,0:T(1,128)} copy(f32[1,512]{1,0:T(1,128)} %shard_map.55) | data formatting | bytes 4096
where the time goes:
time: 97.2 us; the launch traced here: 97 us
  Pallas kernels  94.4 us (97%)
  local copies, waits for them, and re-layouts  2.57 us (3%)
    pallas_call x1, Pallas kernels, shards(): pl.pallas_call(functools.partial(kernel, width, cores), out_shape=jax.Sha...  94.4 us
    unnamed x2, local copies, waits for them, and re-layouts  2.57 us

commit v1 on v0

--- a/solution.py
+++ b/solution.py
@@ -22,7 +22,7 @@
 
 def kernel(
     width, cores, y0_ref, c_hbm, m_hbm, gains_ref, forcing_ref, out_ref,
-    cbuf, mbuf, bt, vt, wa_hi, wa_lo, wb_hi, wb_lo, wc_hi, wc_lo,
+    cbuf, mbuf, bt, vt, w_hi, w_lo,
     x, acc, xs0, xs1, zs, gbuf, fbuf, chain_in, out_in, psend, yv,
     csem, gsend, grecv, vsend, fsend, frecv, chain_send, chain_recv, out_send, out_recv,
 ):
@@ -32,7 +32,7 @@
     steps = (nodes - 1) // 2
     half = out_ref.shape[1]
     window = chain_in.shape[2]
-    tile = min(256, size)
+    tile = min(1024, size)
     devices = lax.axis_size("tm") * cores
     groups = devices // width
     me_tm, me_col = lax.axis_index("tm"), lax.axis_index("col")
@@ -94,7 +94,9 @@
     @pl.when(flat == 0)
     def _():
         gbuf[0] = gains_ref[...]
-        fbuf[0] = forcing_ref[0]
+        own_force = pltpu.make_async_copy(forcing_ref.at[0], fbuf.at[0], csem.at[2])
+        own_force.start()
+        own_force.wait()
 
     row_id = lax.broadcasted_iota(jnp.int32, (rows, tile), 0)
     col_id = lax.broadcasted_iota(jnp.int32, (rows, tile), 1)
@@ -134,33 +136,37 @@
 
     pieces = max(1, size // 128)
 
-    def form(ns, gain, w_hi, w_lo):
+    def form(ns, gain, keep):
+        his, los = [], []
         for k in range(pieces):
             ks = slice(k * size // pieces, (k + 1) * size // pieces)
             w = bt[ks, ns] + gain * vt[ks, ns]
             hi = w.astype(bf16)
-            w_hi[ks, ns] = hi
-            w_lo[ks, ns] = (w - hi.astype(f32)).astype(bf16)
-
-    wa, wb, wc = (wa_hi, wa_lo), (wb_hi, wb_lo), (wc_hi, wc_lo)
+            lo = (w - hi.astype(f32)).astype(bf16)
+            his.append(hi)
+            los.append(lo)
+            if keep:
+                w_hi[ks, ns] = hi
+                w_lo[ks, ns] = lo
+        return jnp.concatenate(his, axis=0), jnp.concatenate(los, axis=0)
 
     def gain_of(slab, node):
         return gbuf[slab][:, node:node + 1]
 
-    @pl.loop(0, size // tile)
-    def _(n):
-        form(pl.ds(pl.multiple_of(n * tile, tile), tile), gain_of(0, 0), *wc)
-
     h = step_size
     push = jnp.logical_and(row_id == 0, is_head)
 
-    def stage(slab, kind, node, w, source, target, following):
+    def stage(slab, kind, node, fresh, keep, source, target):
         @pl.loop(0, size // tile)
         def _(n):
             ns = pl.ds(pl.multiple_of(n * tile, tile), tile)
-            both = jnp.dot(source[...], w[0][:, ns], preferred_element_type=f32)
+            if fresh:
+                hi, lo = form(ns, gain_of(slab, node), keep)
+            else:
+                hi, lo = w_hi[:, ns], w_lo[:, ns]
+            both = jnp.dot(source[...], hi, preferred_element_type=f32)
             k = both[:rows] + both[rows:]
-            k = k + jnp.dot(source[:rows, :], w[1][:, ns], preferred_element_type=f32)
+            k = k + jnp.dot(source[:rows, :], lo, preferred_element_type=f32)
             k = k + jnp.where(push, fbuf[slab, node:node + 1, ns], 0.0)
             now = x[:, ns]
             if kind == 0:
@@ -180,20 +186,15 @@
             hi = arg.astype(bf16)
             target[:rows, ns] = hi
             target[rows:, ns] = (arg - hi.astype(f32)).astype(bf16)
-            if following is not None:
-                form(ns, following[0], *following[1])
 
     @pl.loop(0, slabs)
     def _(slab):
-        after = jnp.minimum(slab + 1, slabs - 1)
         for step in range(steps):
-            w0 = wc if step == 0 else wa
             base = 2 * step
-            last = step == steps - 1
-            stage(slab, 0, base, w0, xs0, xs1, (gain_of(slab, base + 1), wb) if step == 0 else None)
-            stage(slab, 1, base + 1, wb, xs1, xs0, (gain_of(slab, base + 2), wa))
-            stage(slab, 2, base + 1, wb, xs0, xs1, None)
-            stage(slab, 3, base + 2, wa, xs1, xs0, (gain_of(after, 0), wc) if last else (gain_of(slab, base + 3), wb))
+            stage(slab, 0, base, step == 0, False, xs0, xs1)
+            stage(slab, 1, base + 1, True, True, xs1, xs0)
+            stage(slab, 2, base + 1, False, False, xs0, xs1)
+            stage(slab, 3, base + 2, True, step < steps - 1, xs1, xs0)
 
     def start_of(q):
         return q * rows // 128 * 128
@@ -347,12 +348,12 @@
             pl.BlockSpec(memory_space=pl.ANY),
             pl.BlockSpec(memory_space=pl.ANY),
             pl.BlockSpec(memory_space=vmem),
-            pl.BlockSpec(memory_space=vmem),
+            pl.BlockSpec(memory_space=pl.ANY),
         ],
         out_specs=pl.BlockSpec(memory_space=vmem),
         scratch_shapes=[
             mat32, mat32, mat32, mat32,
-            mat16, mat16, mat16, mat16, mat16, mat16,
+            mat16, mat16,
             vmem((rows, size), f32),
             vmem((rows, size), f32),
             vmem((2 * rows, size), bf16),
@@ -364,7 +365,7 @@
             vmem((width + 1, 1, half), f32),
             vmem((slabs, 1, size), f32),
             vmem((1, window), f32),
-            dma((2,)), dma((slabs,)), dma((slabs,)), dma((1,)), dma((1,)), dma((slabs,)),
+            dma((3,)), dma((slabs,)), dma((slabs,)), dma((1,)), dma((1,)), dma((slabs,)),
             dma((width,)), dma((width + 1,)), dma((width,)), dma((width + 1,)),
         ],
         compiler_params=pltpu.CompilerParams(

time: 97.2 us -> 61.5 us (0.63)
  Pallas kernels: 94.4 us -> 58.6 us
    pallas_call x1, Pallas kernels: 94.4 us -> 58.6 us  [shards(): pl.pallas_call(functools.partial(kernel, width, cores), out_shape=jax.Sha...]
where the time goes in v1:
time: 61.5 us; the launch traced here: 61.2 us
  Pallas kernels  58.6 us (95%)
  local copies, waits for them, and re-layouts  2.57 us (4%)
    pallas_call x1, Pallas kernels, shards(): pl.pallas_call(functools.partial(kernel, width, cores), out_shape=jax.Sha...  58.6 us
    unnamed x2, local copies, waits for them, and re-layouts  2.57 us

profile of v1, /device:TPU:25, one launch (start us, length us, event | category | flops | bytes accessed | tf_op | source)
XLA Modules:
  0.0 61.2 jit_solution(14767776724191120437)
XLA Ops:
  0.0 1.3 %copy.6.forcing_ref = f32[1,5,1024]{2,1,0:T(8,128)} copy(f32[1,5,1024]{2,0,1:T(1,128)} %param.9) | data formatting | bytes 40960 | tf_op args[4]
  1.3 58.6 %shard_map.55 = f32[1,512]{1,0:T(1,128)} custom-call(f32[1,1024]{1,0:T(1,128)} %bitcast.1, f32[1024,1024]{1,0:T(8,128)} %c_hbm.1, f32[1024,1024]{1,0:T(8,128)} %m_hbm.1, f32[1,5]{1,0:T(1,128)} %gains_ref.1, f32[1,5,1024]{2,1,0:T(8,128)} %copy.6.forcing_ref), custom_call_target="tpu_custom_call" | custom-call | tf_op jit(solution)/shard_map/pallas_call | solution.py:343
  60.0 1.2 %copy.8 = f32[1,512]{1,0:T(1,128)} copy(f32[1,512]{1,0:T(1,128)} %shard_map.55) | data formatting | bytes 4096
